TPU v7x, 128 devices: a whole 4x4x4 slice. The times are simulated.
128 devices in a mesh: row: 8 (over x_lo, z), col: 16 (over x_hi, y, core).
Axes of the slice: x: 4 (x_hi: 2, x_lo: 2; x = x_hi * 2 + x_lo), y: 4, z: 4, core: 2. Of those that a mesh axis runs over, the one named last changes fastest.
Arguments:
- tokens: bfloat16 [2048, 4096], P('row', 'col'), may hold values from -6 to 6
- norm_gain: float32 [4096], replicated, may hold values from 0.1 to 1.9
- expert_ids: int32 [2048, 2], P('row'), may hold values from 0 to 7, all different within a row; in each aligned block of 256 rows (0 to 255, 256 to 511, ...) at most 128 rows name the same one
- gate_weights: float32 [2048, 2], P('row'), may hold values from 0.1 to 1
- w_gate: bfloat16 [8, 4096, 14336], P('row', None, 'col'), may hold values from -0.09375 to 0.09375
- w_up: bfloat16 [8, 4096, 14336], P('row', None, 'col'), may hold values from -0.09375 to 0.09375
- w_down: bfloat16 [8, 14336, 4096], P('row', 'col'), may hold values from -0.046875 to 0.046875
Outputs:
- layer_output: bfloat16 [2048, 4096], P('row', 'col')
Inputs may be any that keep to these rules, and one draw needn't show every extreme that they name: `expert_ids`: the 2 experts of a token differ. In each aligned block of 256 tokens no expert is chosen by more than 128 tokens, a bound that some block reaches.
All inputs are finite; a program needn't handle non-finite values.
Results may differ from a plain program's by a relative error of at most 0.0043.
Values may be sent and summed in bfloat16 or wider, within the bound.
A program may use at most 128 MiB of HBM per device.

v0:
```python
import jax
import jax.numpy as jnp
from jax import lax
from jax.sharding import Mesh
from jax.sharding import PartitionSpec as P

EXPERTS = 8
CAP = 128
COL = ("chip", "core")


def route_tables(expert_ids, expert_count, capacity):
    token_count = expert_ids.shape[0]
    flat_ids = expert_ids.reshape(-1)
    expert_range = jnp.arange(expert_count, dtype=jnp.int32)
    expert_hits = (flat_ids[:, None] == expert_range[None, :]).astype(jnp.int32)
    earlier = jnp.cumsum(expert_hits, axis=0) - expert_hits
    ranks = jnp.sum(earlier * expert_hits, axis=1)
    slot_index = (flat_ids * capacity + ranks).reshape(token_count, -1)
    slot_ids = jnp.arange(expert_count * capacity, dtype=jnp.int32)
    matches = (slot_index[:, :, None] == slot_ids[None, None, :]).astype(jnp.float32)
    picker = jnp.sum(matches, axis=1)
    return (picker.astype(jnp.bfloat16), slot_index)


def combine_rows(slot_rows, slot_index, gate_weights):
    picked = slot_rows[slot_index]
    return jnp.sum(picked * gate_weights[:, :, None], axis=1)


def swap_cores(value):
    return lax.ppermute(value, "core", perm=[(0, 1), (1, 0)])


def body(tokens, norm_gain, expert_ids, gate_weights, w_gate, w_up, w_down):
    chips = lax.psum(1, "chip")
    width = tokens.shape[1]
    core = lax.axis_index("core")
    block = lax.axis_index("chip") * 2 + core
    values = tokens.astype(jnp.float32)
    squares = lax.psum(jnp.sum(values * values, axis=-1, keepdims=True), COL)
    inverse_norm = lax.rsqrt(squares / (width * chips * 2) + 1e-05)
    gain = lax.dynamic_slice_in_dim(norm_gain, block * width, width)
    normed = (values * inverse_norm * gain).astype(jnp.bfloat16)
    picker, slot_index = route_tables(expert_ids, EXPERTS, CAP)
    packed = jnp.einsum("ts,td->sd", picker, normed, preferred_element_type=jnp.float32).astype(
        jnp.bfloat16
    )
    packed = packed.reshape(EXPERTS, CAP, width)
    arrived = lax.all_to_all(packed, "row", split_axis=0, concat_axis=0, tiled=True)
    arrived = arrived.reshape(EXPERTS * CAP, width)
    mine = lax.all_gather(arrived, "chip", axis=0, tiled=False)
    other = swap_cores(mine)
    pair = jnp.where(core == 0, jnp.stack([mine, other], 1), jnp.stack([other, mine], 1))
    slots = arrived.shape[0]
    widened = jnp.transpose(pair, (2, 0, 1, 3)).reshape(slots, chips * 2 * width)
    gate_part = jnp.dot(widened, w_gate[0], preferred_element_type=jnp.float32)
    up_part = jnp.dot(widened, w_up[0], preferred_element_type=jnp.float32)
    hidden = (jax.nn.silu(gate_part) * up_part).astype(jnp.bfloat16)
    outputs = jnp.dot(hidden, w_down[0], preferred_element_type=jnp.float32)
    split = outputs.reshape(slots, chips, 2, width)
    keep = jnp.where(core == 0, split[:, :, 0], split[:, :, 1])
    give = jnp.where(core == 0, split[:, :, 1], split[:, :, 0])
    summed = keep + swap_cores(give)
    shares = lax.psum_scatter(summed, "chip", scatter_dimension=1, tiled=True)
    shares = shares.reshape(EXPERTS, CAP, width)
    returned = lax.all_to_all(shares, "row", split_axis=0, concat_axis=0, tiled=True)
    mixed = combine_rows(returned.reshape(-1, width), slot_index, gate_weights)
    return (tokens.astype(jnp.float32) + mixed).astype(jnp.bfloat16)


def solution(mesh):
    rows, cols = mesh.devices.shape
    split_mesh = Mesh(mesh.devices.reshape(rows, cols // 2, 2), ("row", "chip", "core"))
    placed = (
        P("row", COL),
        P(),
        P("row", None),
        P("row", None),
        P("row", None, COL),
        P("row", None, COL),
        P("row", COL, None),
    )
    return jax.shard_map(
        body, mesh=split_mesh, in_specs=placed, out_specs=P("row", COL), check_vma=False
    )
```

profile of v0, /device:TPU:0, one launch (start us, length us, event | category | flops | bytes accessed | tf_op | source)
XLA Modules:
  0.0 370.8 jit_solution(8695487437753940584)
XLA Ops:
  6.5 0.0 all-gather.2.cloned.1.call-start
  6.5 0.8 copy.51
  7.4 0.1 eq.48
  7.5 0.1 eq.44
  7.7 1.1 reduce-window.6
  8.8 0.2 slice_reduce_fusion
  9.1 0.1 fusion.17
  9.2 0.1 reduce_sum.39
  9.3 0.1 copy.53
  9.4 0.7 compare_select_fusion
  10.1 0.3 convert_reduce_fusion
  10.4 1.0 fusion.9
  11.4 38.1 %psum.7 = f32[256,1]{0,1:T(1,128)S(1)} all-reduce(f32[256,1]{0,1:T(1,128)S(1)} %bitcast.67), channel_id=1, replica_groups=mesh['row'=8,'chip'=8,'core'=2] {'chip','core'}, use_global_device_ids=true, to_apply=%region_5.6 | all-reduce | flops 256 | bytes 2048 | tf_op jit(solution)/shard_map/psum | solution.py:41
  49.5 0.8 dynamic_slice.3
  50.3 1.3 convolution_convert_fusion
  51.6 13.9 %all_to_all.10 = bf16[8,128,256]{2,1,0:T(8,128)(2,1)} all-to-all(bf16[8,128,256]{2,1,0:T(8,128)(2,1)S(1)} %bitcast.66), channel_id=1, replica_groups=mesh['row'=8,'chip'=8,'core'=2] {'row'}, dimensions={0} | all-to-all | bytes 1048576 | tf_op jit(solution)/shard_map/all_to_all | solution.py:50
  65.5 0.0 all-gather.2.cloned.1.call-update
  65.5 0.0 reduce-scatter.2.cloned.1.call-start
  65.5 67.0 %all-gather.2.cloned.1.call-done = bf16[8,1024,256]{2,1,0:T(8,128)(2,1)} async-done(((bf16[1,1024,256]{2,1,0:T(8,128)(2,1)}), bf16[8,1024,256]{2,1,0:T(8,128)(2,1)}) %all-gather.2.cloned.1.call-update) | async-done | bytes 4194320 | tf_op jit(solution)/shard_map/all_gather | solution.py:52
  132.6 6.4 %copy.54 = bf16[8,1024,256]{1,2,0:T(8,128)(2,1)} copy(bf16[8,1024,256]{2,1,0:T(8,128)(2,1)} %all-gather.2.cloned.1.call-done) | data formatting | bytes 8388608 | tf_op jit(solution)/shard_map/all_gather | solution.py:52
  139.0 0.0 collective-permute-start
  139.0 10.8 %copy.64 = bf16[4096,896]{1,0:T(8,128)(2,1)} copy(bf16[4096,896]{0,1:T(8,128)(2,1)} %bitcast.60) | data formatting | bytes 14680064 | tf_op jit(solution)/shard_map/dot_general | solution.py:60
  149.8 0.0 collective-permute-done
  149.8 7.9 %maximum_select_fusion = bf16[8,2,1024,256]{2,3,1,0:T(8,128)(2,1)S(1)} fusion(bf16[8,1,1024,256]{2,3,1,0:T(8,128)(2,1)} %bitcast.7, bf16[8,1,1024,256]{2,3,1,0:T(8,128)(2,1)} %bitcast.57, pred[]{:T(512)S(6)} %eq.43), kind=kLoop, calls=%fused_computation.1 | loop fusion | flops 12582912 | bytes 16777216 | tf_op jit(solution)/shard_map/jit(_where)/select_n | solution.py:54
  157.8 0.0 slice-start.3
  157.8 0.0 slice-start
  157.8 13.0 %fusion.2 = f32[1024,896]{1,0:T(8,128)S(1)} fusion(bf16[1024,4096]{0,1:T(8,128)(2,1)S(1)} %bitcast.58, bf16[1,4096,896]{2,1,0:T(8,128)(2,1)} %param.12), kind=kOutput, calls=%fused_computation.6 | convolution fusion | flops 7516192768 | bytes 19398656 | tf_op jit(solution)/shard_map/dot_general | solution.py:58
  170.8 0.0 slice-done.2
  170.8 0.0 slice-done.3
  170.9 0.0 slice-start.1
  170.9 11.1 %fusion.4 = f32[1024,896]{1,0:T(8,128)} fusion(bf16[1024,4096]{0,1:T(8,128)(2,1)S(1)} %bitcast.59, bf16[1,4096,896]{2,1,0:T(8,128)(2,1)S(1)} %bitcast.70), kind=kOutput, calls=%fused_computation.8 | convolution fusion | flops 7516192768 | bytes 19398656 | tf_op jit(solution)/shard_map/dot_general | solution.py:57
  182.0 0.0 slice-done.1
  182.0 13.8 %fusion.6 = f32[1024,8,2,256]{3,0,2,1:T(8,128)} fusion(bf16[8,2,256,896]{3,2,1,0:T(8,128)(2,1)S(1)} %bitcast.63, f32[1024,896]{1,0:T(8,128)S(1)} %fusion.2, f32[1024,896]{1,0:T(8,128)} %fusion.4), kind=kOutput, calls=%fused_computation.13 | convolution fusion | flops 7521697792 | bytes 31457280 | tf_op jit(solution)/shard_map/dot_general | solution.py:60
  195.8 10.1 %select_bitcast_fusion = f32[1024,8,256]{2,0,1:T(8,128)} fusion(f32[1024,8,2,256]{3,0,2,1:T(8,128)} %fusion.6, pred[]{:T(512)S(6)} %eq.43), kind=kLoop, calls=%fused_computation.5 | loop fusion | flops 2097152 | bytes 25165824 | tf_op jit(solution)/shard_map/jit(_where)/select_n | solution.py:63
  205.8 0.5 collective-permute-start.1
  206.3 13.0 %collective-permute-done.1 = f32[1024,8,256]{2,0,1:T(8,128)S(1)} collective-permute-done((f32[1024,8,256]{2,0,1:T(8,128)}, f32[1024,8,256]{2,0,1:T(8,128)S(1)}, u32[]{:S(2)}, u32[]{:S(2)}) %collective-permute-start.1) | collective-permute-done | bytes 8388640 | tf_op jit(solution)/shard_map/ppermute | solution.py:32
  219.3 10.0 %fusion.1 = f32[1024,8,256]{2,0,1:T(8,128)} fusion(f32[1024,8,256]{2,0,1:T(8,128)S(1)} %collective-permute-done.1, f32[1024,8,2,256]{3,0,2,1:T(8,128)} %fusion.6, pred[]{:T(512)S(6)} %eq.43), kind=kLoop, calls=%fused_computation.4 | loop fusion | flops 4194304 | bytes 33554432 | tf_op jit(solution)/shard_map/add | solution.py:64
  229.4 0.0 reduce-scatter.2.cloned.1.call-update
  229.4 112.7 %reduce-scatter.2.cloned.1.call-done = f32[1024,1,256]{2,0,1:T(8,128)} async-done(((f32[1024,8,256]{2,0,1:T(8,128)}), f32[1024,1,256]{2,0,1:T(8,128)}) %reduce-scatter.2.cloned.1.call-update) | async-done | bytes 1048592 | tf_op jit(solution)/shard_map/reduce_scatter | solution.py:65
  342.1 4.4 %all-to-all-start.1 = ((f32[8,128,256]{2,1,0:T(8,128)}), f32[8,128,256]{2,1,0:T(8,128)S(1)}, u32[]{:S(2)}, u32[]{:S(2)}) async-start(f32[8,128,256]{2,1,0:T(8,128)} %bitcast.65), calls=%async_computation.2 | async-start | bytes 2097152 | tf_op jit(solution)/shard_map/all_to_all | solution.py:67
  346.5 0.1 copy.61
  346.6 0.1 reshape.53
  346.8 0.1 copy.62
  347.0 13.7 %all-to-all-done.1 = f32[8,128,256]{2,1,0:T(8,128)S(1)} async-done(((f32[8,128,256]{2,1,0:T(8,128)}), f32[8,128,256]{2,1,0:T(8,128)S(1)}, u32[]{:S(2)}, u32[]{:S(2)}) %all-to-all-start.1) | async-done | bytes 1048608 | tf_op jit(solution)/shard_map/all_to_all | solution.py:67
  360.7 1.6 gather_fusion
  362.3 0.3 reshape.52
  362.6 0.7 multiply_reduce_fusion
  363.3 0.7 fusion.12
  (13 shorter events, 0.1 us)
Async XLA Ops:
  6.5 126.0 %all-gather.2.cloned.1.call-start = ((), (), s32[]{:S(2)}) async-start(), calls=%async_computation.3 | async-start | bytes 4718592 | tf_op jit(solution)/shard_map/all_gather | solution.py:52
  65.5 276.6 %reduce-scatter.2.cloned.1.call-start = ((), (), s32[]{:S(2)}) async-start(), calls=%async_computation.4 | async-start | bytes 9437184 | tf_op jit(solution)/shard_map/reduce_scatter | solution.py:65
  139.0 10.8 %collective-permute-start = (bf16[8,1024,256]{1,2,0:T(8,128)(2,1)}, bf16[8,1024,256]{1,2,0:T(8,128)(2,1)}, u32[]{:S(2)}, u32[]{:S(2)}) collective-permute-start(bf16[8,1024,256]{1,2,0:T(8,128)(2,1)} %copy.54), channel_id=1, source_target_pairs={{0,1},{1,0},{2,3},{3,2},{4,5},{5,4},{6,7},{7,6},{8,9},{9,8},{10,11... | collective-permute-start | bytes 12582920 | tf_op jit(solution)/shard_map/ppermute | solution.py:32
  149.8 21.0 %slice-start.2 = ((s8[7340032]{0:T(1024)(128)(4,1)}), s8[4194304]{0:T(1024)(128)(4,1)S(1)}, s32[]{:S(2)}) async-start(s8[7340032]{0:T(1024)(128)(4,1)} %bitcast.69), calls=%async_computation.7 | async-start | bytes 8388608
  157.8 13.1 %slice-start.3 = ((s8[7340032]{0:T(1024)(128)(4,1)}), s8[3145728]{0:T(1024)(128)(4,1)S(1)}, s32[]{:S(2)}) async-start(s8[7340032]{0:T(1024)(128)(4,1)} %bitcast.69), calls=%async_computation.8 | async-start | bytes 6291456
  157.8 24.2 %slice-start = ((s8[7340032]{0:T(1024)(128)(4,1)}), s8[4194304]{0:T(1024)(128)(4,1)S(1)}, s32[]{:S(2)}) async-start(s8[7340032]{0:T(1024)(128)(4,1)} %bitcast.61), calls=%async_computation.5 | async-start | bytes 8388608
  170.9 11.1 %slice-start.1 = ((s8[7340032]{0:T(1024)(128)(4,1)}), s8[3145728]{0:T(1024)(128)(4,1)S(1)}, s32[]{:S(2)}) async-start(s8[7340032]{0:T(1024)(128)(4,1)} %bitcast.61), calls=%async_computation.6 | async-start | bytes 6291456
  205.8 13.5 %collective-permute-start.1 = (f32[1024,8,256]{2,0,1:T(8,128)}, f32[1024,8,256]{2,0,1:T(8,128)S(1)}, u32[]{:S(2)}, u32[]{:S(2)}) collective-permute-start(f32[1024,8,256]{2,0,1:T(8,128)} %select_bitcast_fusion), channel_id=1, source_target_pairs={{0,1},{1,0},{2,3},{3,2},{4,5},{5,4},{6,7},{7,6},{8,9},{9,8},{10,11... | collective-permute-start | bytes 25165832 | tf_op jit(solution)/shard_map/ppermute | solution.py:32
  229.3 117.4 %copy-start.1 = (f32[256,2]{0,1:T(2,128)S(1)}, f32[256,2]{0,1:T(2,128)}, u32[]{:S(2)}) copy-start(f32[256,2]{0,1:T(2,128)} %param.10) | copy-start | bytes 6148
  229.3 134.0 %copy-start = (bf16[256,256]{1,0:T(8,128)(2,1)S(1)}, bf16[256,256]{1,0:T(8,128)(2,1)}, u32[]{:S(2)}) copy-start(bf16[256,256]{1,0:T(8,128)(2,1)} %param.7) | copy-start | bytes 393220
  342.1 18.6 %all-to-all-start.1 = ((f32[8,128,256]{2,1,0:T(8,128)}), f32[8,128,256]{2,1,0:T(8,128)S(1)}, u32[]{:S(2)}, u32[]{:S(2)}) async-start(f32[8,128,256]{2,1,0:T(8,128)} %bitcast.65), calls=%async_computation.2 | async-start | bytes 2097152 | tf_op jit(solution)/shard_map/all_to_all | solution.py:67
Sparse Core Ops, SparseCore 0:
  65.6 66.8 all-gather.1
  229.5 112.5 reduce-scatter.1
where the time goes:
time: 372 us; the launch traced here: 371 us
  waiting for transfers between devices  206 us (55%)
  blocking collectives  52 us (14%)
  matrix products  39.2 us (11%)
  other arithmetic  32.7 us (9%)
  local copies, waits for them, and re-layouts  21.9 us (6%)
  between operations  13.6 us (4%)
  starting transfers between devices  4.98 us (1%)
    reduce_scatter x1, waiting for transfers between devices, body(): shares = lax.psum_scatter(summed, 'chip', scatter_dimension=1, tiled=True)  113 us
    all_gather x1, waiting for transfers between devices, body(): mine = lax.all_gather(arrived, 'chip', axis=0, tiled=False)  67 us
    psum x1, blocking collectives, body(): squares = lax.psum(jnp.sum(values * values, axis=-1, keepdims=True), COL)  38.1 us
    all_to_all x1, blocking collectives, body(): lax.all_to_all(packed, 'row', split_axis=0, concat_axis=0, tiled=True)  13.9 us
    dot_general x1, matrix products, body(): outputs = jnp.dot(hidden, w_down[0], preferred_element_type=jnp.float32)  13.8 us
    all_to_all x1, waiting for transfers between devices, body(): lax.all_to_all(shares, 'row', split_axis=0, concat_axis=0, tiled=True)  13.7 us
    dot_general x1, matrix products, body(): up_part = jnp.dot(widened, w_up[0], preferred_element_type=jnp.float32)  13 us
    ppermute x2, waiting for transfers between devices, swap_cores(): return lax.ppermute(value, 'core', perm=[(0, 1), (1, 0)])  13 us
  transfers between devices with their start and end apart: 5, of which 4 were waited for; matrix products, arithmetic and copies ran while one was open for 3% of the time, Pallas kernels for 0%

commit v1 on v0

--- a/solution.py
+++ b/solution.py
@@ -38,7 +38,7 @@
     core = lax.axis_index("core")
     block = lax.axis_index("chip") * 2 + core
     values = tokens.astype(jnp.float32)
-    squares = lax.psum(jnp.sum(values * values, axis=-1, keepdims=True), COL)
+    squares = jnp.sum(lax.all_gather(jnp.sum(values * values, axis=-1, keepdims=True), COL), axis=0)
     inverse_norm = lax.rsqrt(squares / (width * chips * 2) + 1e-05)
     gain = lax.dynamic_slice_in_dim(norm_gain, block * width, width)
     normed = (values * inverse_norm * gain).astype(jnp.bfloat16)

time: 372 us -> 360 us (0.968)
  blocking collectives: 52 us -> 40.2 us
    psum x1 -> x0, blocking collectives: 38.1 us -> none  [body(): squares = lax.psum(jnp.sum(values * values, axis=-1, keepdims=True), COL)]
    all_gather x0 -> x1, blocking collectives: none -> 24.5 us  [body(): lax.all_gather(jnp.sum(values * values, axis=-1, keepdims=True), COL)]
where the time goes in v1:
time: 360 us; the launch traced here: 359 us
  waiting for transfers between devices  206 us (57%)
  blocking collectives  40.2 us (11%)
  matrix products  39.2 us (11%)
  other arithmetic  32.7 us (9%)
  local copies, waits for them, and re-layouts  21.9 us (6%)
  between operations  13.6 us (4%)
  starting transfers between devices  4.99 us (1%)
    reduce_scatter x1, waiting for transfers between devices, body(): shares = lax.psum_scatter(summed, 'chip', scatter_dimension=1, tiled=True)  113 us
    all_gather x1, waiting for transfers between devices, body(): mine = lax.all_gather(arrived, 'chip', axis=0, tiled=False)  67.1 us
    all_gather x1, blocking collectives, body(): lax.all_gather(jnp.sum(values * values, axis=-1, keepdims=True), COL)  24.5 us
    all_to_all x1, blocking collectives, body(): lax.all_to_all(packed, 'row', split_axis=0, concat_axis=0, tiled=True)  15.7 us
    dot_general x1, matrix products, body(): outputs = jnp.dot(hidden, w_down[0], preferred_element_type=jnp.float32)  13.8 us
    all_to_all x1, waiting for transfers between devices, body(): lax.all_to_all(shares, 'row', split_axis=0, concat_axis=0, tiled=True)  13.8 us
    dot_general x1, matrix products, body(): up_part = jnp.dot(widened, w_up[0], preferred_element_type=jnp.float32)  13 us
    ppermute x2, waiting for transfers between devices, swap_cores(): return lax.ppermute(value, 'core', perm=[(0, 1), (1, 0)])  13 us
  transfers between devices with their start and end apart: 5, of which 4 were waited for; matrix products, arithmetic and copies ran while one was open for 3% of the time, Pallas kernels for 0%

profile of v1, /device:TPU:0, one launch (start us, length us, event | category | flops | bytes accessed | tf_op | source)
XLA Modules:
  0.0 359.1 jit_solution(1768835045597545297)
XLA Ops:
  6.5 0.0 all-gather.4.cloned.1.call-start
  6.5 0.8 copy.51
  7.4 0.1 eq.48
  7.5 0.1 eq.44
  7.7 1.1 reduce-window.6
  8.8 0.2 slice_reduce_fusion
  9.1 0.1 fusion.17
  9.2 0.1 reduce_sum.48
  9.3 0.1 copy.53
  9.4 0.7 compare_select_fusion
  10.1 0.3 convert_reduce_fusion
  10.4 1.0 fusion.9
  11.4 24.5 %all-gather.1 = f32[16,1,256]{2,1,0:T(1,128)S(1)} all-gather(f32[1,1,256]{2,1,0:T(1,128)S(1)} %bitcast.66), channel_id=2, replica_groups=mesh['row'=8,'chip'=8,'core'=2] {'chip','core'}, dimensions={0}, use_global_device_ids=true | all-gather | bytes 17408 | tf_op jit(solution)/shard_map/all_gather | solution.py:41
  35.9 0.8 dynamic_slice.3
  36.7 1.3 convolution_convert_fusion
  38.0 15.7 %all_to_all.10 = bf16[8,128,256]{2,1,0:T(8,128)(2,1)} all-to-all(bf16[8,128,256]{2,1,0:T(8,128)(2,1)S(1)} %bitcast.65), channel_id=1, replica_groups=mesh['row'=8,'chip'=8,'core'=2] {'row'}, dimensions={0} | all-to-all | bytes 1048576 | tf_op jit(solution)/shard_map/all_to_all | solution.py:50
  53.7 0.0 all-gather.4.cloned.1.call-update
  53.7 0.0 reduce-scatter.2.cloned.1.call-start
  53.8 67.1 %all-gather.4.cloned.1.call-done = bf16[8,1024,256]{2,1,0:T(8,128)(2,1)} async-done(((bf16[1,1024,256]{2,1,0:T(8,128)(2,1)}), bf16[8,1024,256]{2,1,0:T(8,128)(2,1)}) %all-gather.4.cloned.1.call-update) | async-done | bytes 4194320 | tf_op jit(solution)/shard_map/all_gather | solution.py:52
  120.8 6.4 %copy.54 = bf16[8,1024,256]{1,2,0:T(8,128)(2,1)} copy(bf16[8,1024,256]{2,1,0:T(8,128)(2,1)} %all-gather.4.cloned.1.call-done) | data formatting | bytes 8388608 | tf_op jit(solution)/shard_map/all_gather | solution.py:52
  127.3 0.0 collective-permute-start
  127.3 10.8 %copy.64 = bf16[4096,896]{1,0:T(8,128)(2,1)} copy(bf16[4096,896]{0,1:T(8,128)(2,1)} %bitcast.59) | data formatting | bytes 14680064 | tf_op jit(solution)/shard_map/dot_general | solution.py:60
  138.1 0.0 collective-permute-done
  138.1 7.9 %maximum_select_fusion = bf16[8,2,1024,256]{2,3,1,0:T(8,128)(2,1)S(1)} fusion(bf16[8,1,1024,256]{2,3,1,0:T(8,128)(2,1)} %bitcast.6, bf16[8,1,1024,256]{2,3,1,0:T(8,128)(2,1)} %bitcast.56, pred[]{:T(512)S(6)} %eq.43), kind=kLoop, calls=%fused_computation.1 | loop fusion | flops 12582912 | bytes 16777216 | tf_op jit(solution)/shard_map/jit(_where)/select_n | solution.py:54
  146.0 0.0 slice-start.3
  146.1 0.0 slice-start
  146.1 13.0 %fusion.2 = f32[1024,896]{1,0:T(8,128)S(1)} fusion(bf16[1024,4096]{0,1:T(8,128)(2,1)S(1)} %bitcast.57, bf16[1,4096,896]{2,1,0:T(8,128)(2,1)} %param.12), kind=kOutput, calls=%fused_computation.6 | convolution fusion | flops 7516192768 | bytes 19398656 | tf_op jit(solution)/shard_map/dot_general | solution.py:58
  159.1 0.0 slice-done.2
  159.1 0.0 slice-done.3
  159.1 0.0 slice-start.1
  159.1 11.1 %fusion.4 = f32[1024,896]{1,0:T(8,128)} fusion(bf16[1024,4096]{0,1:T(8,128)(2,1)S(1)} %bitcast.58, bf16[1,4096,896]{2,1,0:T(8,128)(2,1)S(1)} %bitcast.68), kind=kOutput, calls=%fused_computation.8 | convolution fusion | flops 7516192768 | bytes 19398656 | tf_op jit(solution)/shard_map/dot_general | solution.py:57
  170.2 0.0 slice-done.1
  170.2 13.8 %fusion.6 = f32[1024,8,2,256]{3,0,2,1:T(8,128)} fusion(bf16[8,2,256,896]{3,2,1,0:T(8,128)(2,1)S(1)} %bitcast.62, f32[1024,896]{1,0:T(8,128)S(1)} %fusion.2, f32[1024,896]{1,0:T(8,128)} %fusion.4), kind=kOutput, calls=%fused_computation.13 | convolution fusion | flops 7521697792 | bytes 31457280 | tf_op jit(solution)/shard_map/dot_general | solution.py:60
  184.0 10.1 %select_bitcast_fusion = f32[1024,8,256]{2,0,1:T(8,128)} fusion(f32[1024,8,2,256]{3,0,2,1:T(8,128)} %fusion.6, pred[]{:T(512)S(6)} %eq.43), kind=kLoop, calls=%fused_computation.5 | loop fusion | flops 2097152 | bytes 25165824 | tf_op jit(solution)/shard_map/jit(_where)/select_n | solution.py:63
  194.1 0.5 collective-permute-start.1
  194.6 13.0 %collective-permute-done.1 = f32[1024,8,256]{2,0,1:T(8,128)S(1)} collective-permute-done((f32[1024,8,256]{2,0,1:T(8,128)}, f32[1024,8,256]{2,0,1:T(8,128)S(1)}, u32[]{:S(2)}, u32[]{:S(2)}) %collective-permute-start.1) | collective-permute-done | bytes 8388640 | tf_op jit(solution)/shard_map/ppermute | solution.py:32
  207.6 10.0 %fusion.1 = f32[1024,8,256]{2,0,1:T(8,128)} fusion(f32[1024,8,256]{2,0,1:T(8,128)S(1)} %collective-permute-done.1, f32[1024,8,2,256]{3,0,2,1:T(8,128)} %fusion.6, pred[]{:T(512)S(6)} %eq.43), kind=kLoop, calls=%fused_computation.4 | loop fusion | flops 4194304 | bytes 33554432 | tf_op jit(solution)/shard_map/add | solution.py:64
  217.6 0.0 reduce-scatter.2.cloned.1.call-update
  217.6 112.6 %reduce-scatter.2.cloned.1.call-done = f32[1024,1,256]{2,0,1:T(8,128)} async-done(((f32[1024,8,256]{2,0,1:T(8,128)}), f32[1024,1,256]{2,0,1:T(8,128)}) %reduce-scatter.2.cloned.1.call-update) | async-done | bytes 1048592 | tf_op jit(solution)/shard_map/reduce_scatter | solution.py:65
  330.3 4.4 %all-to-all-start.1 = ((f32[8,128,256]{2,1,0:T(8,128)}), f32[8,128,256]{2,1,0:T(8,128)S(1)}, u32[]{:S(2)}, u32[]{:S(2)}) async-start(f32[8,128,256]{2,1,0:T(8,128)} %bitcast.64), calls=%async_computation.2 | async-start | bytes 2097152 | tf_op jit(solution)/shard_map/all_to_all | solution.py:67
  334.7 0.1 copy.61
  334.9 0.1 reshape.62
  335.0 0.1 copy.62
  335.2 13.8 %all-to-all-done.1 = f32[8,128,256]{2,1,0:T(8,128)S(1)} async-done(((f32[8,128,256]{2,1,0:T(8,128)}), f32[8,128,256]{2,1,0:T(8,128)S(1)}, u32[]{:S(2)}, u32[]{:S(2)}) %all-to-all-start.1) | async-done | bytes 1048608 | tf_op jit(solution)/shard_map/all_to_all | solution.py:67
  348.9 1.6 gather_fusion
  350.5 0.3 reshape.61
  350.8 0.7 multiply_reduce_fusion
  351.5 0.7 fusion.12
  (14 shorter events, 0.1 us)
Async XLA Ops:
  6.5 114.3 %all-gather.4.cloned.1.call-start = ((), (), s32[]{:S(2)}) async-start(), calls=%async_computation.3 | async-start | bytes 4718592 | tf_op jit(solution)/shard_map/all_gather | solution.py:52
  53.7 276.6 %reduce-scatter.2.cloned.1.call-start = ((), (), s32[]{:S(2)}) async-start(), calls=%async_computation.4 | async-start | bytes 9437184 | tf_op jit(solution)/shard_map/reduce_scatter | solution.py:65
  127.3 10.8 %collective-permute-start = (bf16[8,1024,256]{1,2,0:T(8,128)(2,1)}, bf16[8,1024,256]{1,2,0:T(8,128)(2,1)}, u32[]{:S(2)}, u32[]{:S(2)}) collective-permute-start(bf16[8,1024,256]{1,2,0:T(8,128)(2,1)} %copy.54), channel_id=1, source_target_pairs={{0,1},{1,0},{2,3},{3,2},{4,5},{5,4},{6,7},{7,6},{8,9},{9,8},{10,11... | collective-permute-start | bytes 12582920 | tf_op jit(solution)/shard_map/ppermute | solution.py:32
  138.1 21.0 %slice-start.2 = ((s8[7340032]{0:T(1024)(128)(4,1)}), s8[4194304]{0:T(1024)(128)(4,1)S(1)}, s32[]{:S(2)}) async-start(s8[7340032]{0:T(1024)(128)(4,1)} %bitcast.67), calls=%async_computation.7 | async-start | bytes 8388608
  146.0 13.1 %slice-start.3 = ((s8[7340032]{0:T(1024)(128)(4,1)}), s8[3145728]{0:T(1024)(128)(4,1)S(1)}, s32[]{:S(2)}) async-start(s8[7340032]{0:T(1024)(128)(4,1)} %bitcast.67), calls=%async_computation.8 | async-start | bytes 6291456
  146.1 24.2 %slice-start = ((s8[7340032]{0:T(1024)(128)(4,1)}), s8[4194304]{0:T(1024)(128)(4,1)S(1)}, s32[]{:S(2)}) async-start(s8[7340032]{0:T(1024)(128)(4,1)} %bitcast.60), calls=%async_computation.5 | async-start | bytes 8388608
  159.1 11.1 %slice-start.1 = ((s8[7340032]{0:T(1024)(128)(4,1)}), s8[3145728]{0:T(1024)(128)(4,1)S(1)}, s32[]{:S(2)}) async-start(s8[7340032]{0:T(1024)(128)(4,1)} %bitcast.60), calls=%async_computation.6 | async-start | bytes 6291456
  194.1 13.5 %collective-permute-start.1 = (f32[1024,8,256]{2,0,1:T(8,128)}, f32[1024,8,256]{2,0,1:T(8,128)S(1)}, u32[]{:S(2)}, u32[]{:S(2)}) collective-permute-start(f32[1024,8,256]{2,0,1:T(8,128)} %select_bitcast_fusion), channel_id=1, source_target_pairs={{0,1},{1,0},{2,3},{3,2},{4,5},{5,4},{6,7},{7,6},{8,9},{9,8},{10,11... | collective-permute-start | bytes 25165832 | tf_op jit(solution)/shard_map/ppermute | solution.py:32
  217.6 117.4 %copy-start.1 = (f32[256,2]{0,1:T(2,128)S(1)}, f32[256,2]{0,1:T(2,128)}, u32[]{:S(2)}) copy-start(f32[256,2]{0,1:T(2,128)} %param.10) | copy-start | bytes 6148
  217.6 133.9 %copy-start = (bf16[256,256]{1,0:T(8,128)(2,1)S(1)}, bf16[256,256]{1,0:T(8,128)(2,1)}, u32[]{:S(2)}) copy-start(bf16[256,256]{1,0:T(8,128)(2,1)} %param.7) | copy-start | bytes 393220
  330.3 18.7 %all-to-all-start.1 = ((f32[8,128,256]{2,1,0:T(8,128)}), f32[8,128,256]{2,1,0:T(8,128)S(1)}, u32[]{:S(2)}, u32[]{:S(2)}) async-start(f32[8,128,256]{2,1,0:T(8,128)} %bitcast.64), calls=%async_computation.2 | async-start | bytes 2097152 | tf_op jit(solution)/shard_map/all_to_all | solution.py:67
Sparse Core Ops, SparseCore 0:
  53.8 66.9 all-gather.3
  217.8 112.4 reduce-scatter.1
